TPU v7x, 32 devices: a whole 2x2x4 slice. The times are simulated.
32 devices in a mesh: band: 2 (over core), grid: 16 (over z, y, x).
Axes of the slice: x: 2, y: 2, z: 4, core: 2. Of those that a mesh axis runs over, the one named last changes fastest.
Arguments:
- coefficients: float32 [4, 2, 128, 128, 128], P('band', None, 'grid'), may hold values from -0.01171875 to 0.01171875
- potential: float32 [128, 128, 128], P('grid'), may hold values from -3 to 3
- external: float32 [128, 128, 128], P('grid'), may hold values from -6 to 6
- core_density: float32 [128, 128, 128], P('grid'), may hold values from 0.05 to 0.5
- rotations: float32 [2, 4, 2], P(None, 'band'), may hold values from -2 to 3
- mlp_in: float32 [3, 32], replicated, may hold values from -4 to 4
- mlp_out: float32 [32], replicated, may hold values from -0.4 to 0.4
Outputs:
- new_coefficients: float32 [4, 2, 128, 128, 128], P('band', None, 'grid')
- new_potential: float32 [128, 128, 128], P('grid')
All inputs are finite; a program needn't handle non-finite values.
Results may differ from a plain program's by a relative error of at most 0.0003.
Values sent between devices are 32-bit elements; how exact they have to be, the bound alone decides.
A program may use at most 64 MiB of HBM per device.

v0:
```python
import functools
import math

import jax
import jax.numpy as jnp
import numpy as np
from jax import lax
from jax.experimental import pallas as pl
from jax.experimental.pallas import tpu as pltpu
from jax.sharding import PartitionSpec as P

MESH = pl.DeviceIdType.MESH
F32 = jnp.float32
BF16 = jnp.bfloat16

step_size = 0.2
epsilon = 1e-06
spacing = 0.58
kinetic_scale = 0.5 * (2.0 * math.pi / spacing) ** 2
coulomb_scale = spacing * spacing / math.pi
gradient_scale = 2.0 * math.pi / spacing
reduced_scale = 2.0 * (3.0 * math.pi * math.pi) ** (1.0 / 3.0)
exchange_scale = (3.0 / math.pi) ** (1.0 / 3.0)


def halves(table):
    table = np.asarray(table, np.float32)
    high = table.astype(BF16)
    low = (table - high.astype(np.float32)).astype(BF16)
    return np.stack([high, low])


def split(value):
    high = value.astype(BF16)
    return high, (value - high.astype(F32)).astype(BF16)


def dot(a, b):
    return jnp.dot(a, b, preferred_element_type=F32)


def table_left(table, value):
    high, low = split(value)
    return dot(table[0], high) + (dot(table[0], low) + dot(table[1], high))


def table_right(value, table):
    high, low = split(value)
    return dot(high, table[0]) + (dot(low, table[0]) + dot(high, table[1]))


def band_tables(n, bands, points):
    half = points // 2
    slots = half // n
    keep = np.arange(half)
    keep = np.where(keep < half // 2, keep, keep - half)
    cell = np.arange(points)
    angle = 2.0 * np.pi * ((keep[:, None] * cell[None, :]) % points) / points
    cos, sin = np.cos(angle), np.sin(angle)
    top = 2.0 * np.pi * ((half // 2 * cell) % points) / points
    ctop, stop = np.cos(top), np.sin(top)
    y_out = np.concatenate([cos.T, sin.T], 1)
    y_in = np.concatenate([cos, sin], 1)
    z_out = np.block([[cos, sin], [-sin, cos]])
    z_in = np.block([[cos.T, -sin.T], [sin.T, cos.T]])
    rows = bands * half
    x_cos = np.zeros((bands, points, n, bands, slots))
    x_sin = np.zeros_like(x_cos)
    for b in range(bands):
        x_cos[b, :, :, b] = cos.T.reshape(points, n, slots)
        x_sin[b, :, :, b] = sin.T.reshape(points, n, slots)
    x_cos = x_cos.reshape(bands * points, rows)
    x_sin = x_sin.reshape(bands * points, rows)
    x_out = np.concatenate([x_cos, x_sin], 1)
    extra = np.zeros((2, 8, bands * points))
    for b in range(bands):
        extra[0, b, b * points : (b + 1) * points] = ctop
        extra[1, b, b * points : (b + 1) * points] = stop
    x_in = np.stack([np.concatenate([x_cos.T, extra[0]]), np.concatenate([x_sin.T, extra[1]])])
    ones, zeros = np.ones(points), np.zeros(points)
    point_out = np.zeros((3, points, 2 * points))
    point_in = np.zeros((3, 2 * points, points))
    for i, (c, s) in enumerate(((ones, zeros), (ctop, stop), (ones, zeros))):
        point_out[i, i + 1] = np.concatenate([c, s])
        point_out[i, half + i + 1] = np.concatenate([-s, c])
        point_in[i, :, i + 1] = np.concatenate([c, s])
        point_in[i, :, half + i + 1] = np.concatenate([-s, c])
    return [halves(t) for t in (y_out, y_in, z_out, z_in, x_out, x_in[0], x_in[1])] + [
        np.moveaxis(halves(point_out), 1, 0),
        np.moveaxis(halves(point_in), 1, 0),
        np.stack([ctop, stop]).astype(np.float32)[:, :, None],
    ]


def band_kernel(
    n, peers, bands, points, iters,
    packed, special, mask, kinetic, potential, core, rotations,
    y_out, y_in, z_out, z_in, x_out, x_in_c, x_in_s, point_out, point_in, phase, y_phase,
    new_out, special_out, density_out,
    current, applied, sent, got, grams, grams_got, levels_r, levels_i, mixed,
    special_got, part, part_got, send_sem, recv_sem, gram_send, gram_recv, first_sem, last_sem, dens_sem,
):
    me = lax.axis_index("grid")
    band = lax.axis_index("band")
    half = points // 2
    slots = half // n
    planes = points // n
    rows = bands * half
    home = n // 2
    high_owner = (half // 2) // planes

    def at(grid):
        return {"band": band, "grid": grid}

    barrier = pltpu.get_barrier_semaphore()

    @pl.loop(1, n)
    def _(i):
        pl.semaphore_signal(barrier, inc=1, device_id=at(lax.rem(me + i, n)), device_id_type=MESH)

    for i in range(1, peers):
        pl.semaphore_signal(
            barrier, inc=1, device_id={"band": lax.rem(band + i, peers), "grid": me}, device_id_type=MESH
        )
    pl.semaphore_wait(barrier, n - 1 + peers - 1)

    def plane_of(device):
        slot = device * slots
        return jnp.where(slot < half // 2, slot, slot + half)

    def first_copy(target):
        start = plane_of(target)
        return pltpu.make_async_remote_copy(
            src_ref=packed.at[:, pl.ds(lax.rem(start, planes), slots)],
            dst_ref=current,
            send_sem=first_sem.at[5 + lax.rem(start, planes) // slots],
            recv_sem=first_sem.at[1],
            device_id=at(target),
            device_id_type=MESH,
        )

    def first_own():
        return pltpu.make_async_copy(
            packed.at[:, pl.ds(lax.rem(plane_of(me), planes), slots)], current, first_sem.at[1]
        )

    def point_copy(place):
        return pltpu.make_async_remote_copy(
            src_ref=special,
            dst_ref=special_got.at[place],
            send_sem=first_sem.at[place * 2],
            recv_sem=first_sem.at[3 + place],
            device_id=at(home),
            device_id_type=MESH,
        )

    source = plane_of(me) // planes

    @pl.when(source == me)
    def _():
        first_own().start()

    @pl.loop(0, n)
    def _(target):
        @pl.when(jnp.logical_and(plane_of(target) // planes == me, target != me))
        def _():
            first_copy(target).start()

    @pl.when(me == 0)
    def _():
        point_copy(0).start()

    @pl.when(me == high_owner)
    def _():
        point_copy(1).start()

    @pl.loop(0, n)
    def _(target):
        @pl.when(jnp.logical_and(plane_of(target) // planes == me, target != me))
        def _():
            first_copy(target).wait_send()

    @pl.when(me == 0)
    def _():
        point_copy(0).wait_send()

    @pl.when(me == high_owner)
    def _():
        point_copy(1).wait_send()

    @pl.when(source == me)
    def _():
        first_own().wait()

    @pl.when(source != me)
    def _():
        first_copy(me).wait_recv()

    @pl.when(me == home)
    def _():
        point_copy(0).wait_recv()
        point_copy(1).wait_recv()
        for b in range(bands):
            current[b, 0, 0:8, :] = current[b, 0, 0:8, :] * mask[0, 0:8, :] * special[0, 8:16, :] + (
                special_got[0, b, 0:8, :] + special_got[1, b, 0:8, :]
            )

    for b in range(bands):
        current[b] = current[b] * mask[...]

    lanes = lax.broadcasted_iota(jnp.int32, (1, points), 1)
    sign = jnp.where(lanes < half, -1.0, 1.0).astype(F32)
    alone = jnp.where(lax.rem(lanes, half) == 0, 1.0, 0.0).astype(F32)

    def turn(value):
        return pltpu.roll(value, half, 1) * sign

    def exchange(stage, with_gram):
        def copies(target, origin):
            found = [
                pltpu.make_async_remote_copy(
                    src_ref=sent.at[stage, target],
                    dst_ref=got.at[stage, origin],
                    send_sem=send_sem.at[stage, target],
                    recv_sem=recv_sem.at[stage, origin],
                    device_id=at(target),
                    device_id_type=MESH,
                )
            ]
            if with_gram is not None:
                found.append(
                    pltpu.make_async_remote_copy(
                        src_ref=grams.at[with_gram],
                        dst_ref=grams_got.at[with_gram, origin],
                        send_sem=gram_send.at[with_gram, target],
                        recv_sem=gram_recv.at[with_gram, origin],
                        device_id=at(target),
                        device_id_type=MESH,
                    )
                )
            return found

        @pl.loop(1, n)
        def _(i):
            for copy in copies(lax.rem(me + i, n), me):
                copy.start()

        own = pltpu.make_async_copy(sent.at[stage, me], got.at[stage, me], recv_sem.at[stage, me])
        own.start()
        if with_gram is not None:
            mine = pltpu.make_async_copy(
                grams.at[with_gram], grams_got.at[with_gram, me], gram_recv.at[with_gram, me]
            )
            mine.start()
            mine.wait()
        own.wait()

        @pl.loop(1, n)
        def _(i):
            for copy in copies(lax.rem(me + i, n), me):
                copy.wait_send()
            origin = lax.rem(me + n - i, n)
            for copy in copies(origin, origin):
                copy.wait_recv()

    def y_outward(source_ref, stage):
        for b in range(bands):
            for x in range(slots):
                value = source_ref[b, x]
                full = table_left(y_out, jnp.concatenate([value, turn(value)], 0))
                sent[stage, :, b, x] = full.reshape(n, planes, points)

    def y_inward(stage, b, x):
        value = got[stage, :, b, x].reshape(points, points)
        return table_left(y_in, jnp.concatenate([value, -turn(value)], 0))

    def swapped(value, s):
        return jnp.concatenate([s * value[:, points:], -s * value[:, :points]], 1)

    y_phase_c = y_phase[0]
    y_phase_s = y_phase[1]

    def space(y_action):
        points_x, points_row = [], []
        for b in range(bands):
            row = mixed[home, b, 0]
            points_x.append(table_right(row, point_out[0]))
            along_z = table_right(row, point_out[1])
            along_y = table_right(row, point_out[2])
            points_row.append(along_z + along_y * y_phase_c + swapped(along_y, -1.0) * y_phase_s)
            mixed[home, b, 0] = row * alone
        levels = table_right(mixed[...].reshape(rows * planes, points), z_out)
        levels_r[0 : rows * planes, :] = levels[:, :points]
        levels_i[0 : rows * planes, :] = levels[:, points:]
        for y in range(planes):
            real = levels_r[pl.ds(y, rows, stride=planes), :]
            imag = levels_i[pl.ds(y, rows, stride=planes), :]
            stacked = jnp.concatenate(
                [jnp.concatenate([real, imag], 1), jnp.concatenate([-imag, real], 1)], 0
            )
            wave = table_left(x_out, stacked)
            found = []
            for b in range(bands):
                at_x = points_x[b][y : y + 1]
                found.append(
                    wave[b * points : (b + 1) * points]
                    + phase[0] * at_x
                    + phase[1] * swapped(at_x, -1.0)
                    + points_row[b][y : y + 1]
                )
            y_action(y, found)

    def spectrum(stage):
        def action(y, found):
            field = potential[y]
            product = jnp.concatenate([f * jnp.concatenate([field, field], 1) for f in found], 0)
            slotted = table_left(x_in_c, product) + table_left(x_in_s, swapped(product, 1.0))
            levels_r[pl.ds(y, rows + 8, stride=planes), :] = slotted[:, :points]
            levels_i[pl.ds(y, rows + 8, stride=planes), :] = slotted[:, points:]

        space(action)
        both = jnp.concatenate([levels_r[...], levels_i[...]], 1)
        found = table_right(both[0 : rows * planes], z_in).reshape(n, bands, slots, planes, points)
        sent[stage] = found
        for b in range(bands):
            start = (rows + b) * planes
            top = both[start : start + planes]
            zero = both[b * slots * planes : b * slots * planes + planes]
            last = table_right(zero, point_in[2])
            last = last * y_phase_c - turn(last) * y_phase_s
            sent[stage, home, b, 0] = (
                sent[stage, home, b, 0] * alone
                + table_right(top, point_in[0])
                + table_right(zero, point_in[1])
                + last
            )

    def pairs():
        return [(i, j) for i in range(bands) for j in range(bands)]

    def mixing(which, turn_at):
        total = jnp.sum(jnp.sum(grams_got[which], 0), 1, keepdims=True)
        square = bands * bands
        cc = {ij: total[k : k + 1] for k, ij in enumerate(pairs())}
        ca = {ij: total[square + k : square + k + 1] for k, ij in enumerate(pairs())}
        aa = {ij: total[2 * square + k : 2 * square + k + 1] for k, ij in enumerate(pairs())}
        factor = [1.0 + step_size * (ca[i, i] / (cc[i, i] + epsilon)) for i in range(bands)]
        moved = {
            (i, j): factor[i] * factor[j] * cc[i, j]
            - step_size * (factor[i] * ca[i, j] + factor[j] * ca[j, i])
            + step_size * step_size * aa[i, j]
            for i, j in pairs()
        }
        weights = []
        for b in range(bands):
            r = [rotations[turn_at, b, c] for c in range(bands)]
            length = sum(r[i] * r[j] * moved[i, j] for i, j in pairs())
            scale = lax.rsqrt(jnp.maximum(length, 0.0) + epsilon)
            weights.append([(scale * r[c] * factor[c], scale * r[c] * (-step_size)) for c in range(bands)])
        return weights

    y_outward(current, 0)
    exchange(0, None)
    mixed[...] = got[0]
    stage = 0
    for t in range(iters):
        spectrum(stage + 1)
        exchange(stage + 1, None)
        for b in range(bands):
            for x in range(slots):
                applied[b, x] = mask[x] * (
                    kinetic[x] * current[b, x] + y_inward(stage + 1, b, x) * (1.0 / points**3)
                )
        for k, (i, j) in enumerate(pairs()):
            for q, (u, v) in enumerate(((current, current), (current, applied), (applied, applied))):
                product = jnp.sum((u[i] * v[j]).reshape(slots * half, points), 0, keepdims=True)
                grams[t, q * bands * bands + k : q * bands * bands + k + 1, :] = product
        y_outward(applied, stage + 2)
        exchange(stage + 2, t)
        weights = mixing(t, t)
        old = [got[0, :, b] for b in range(bands)]
        new_mixed, new_current = [], []
        for b in range(bands):
            new_mixed.append(
                sum(weights[b][c][0] * old[c] + weights[b][c][1] * got[stage + 2, :, c] for c in range(bands))
            )
            new_current.append(
                sum(weights[b][c][0] * current[c] + weights[b][c][1] * applied[c] for c in range(bands))
            )
        for b in range(bands):
            current[b] = new_current[b]
            mixed[:, b] = new_mixed[b]
            got[0, :, b] = new_mixed[b]
        stage += 2

    def last_arrival(origin):
        place = new_out.at[:, pl.ds(lax.rem(plane_of(origin), planes), slots)]
        return pltpu.make_async_remote_copy(
            src_ref=current,
            dst_ref=place,
            send_sem=last_sem.at[0],
            recv_sem=last_sem.at[4 + lax.rem(plane_of(origin), planes) // slots],
            device_id=at(origin),
            device_id_type=MESH,
        )

    def last_sent():
        return pltpu.make_async_remote_copy(
            src_ref=current,
            dst_ref=new_out.at[:, pl.ds(lax.rem(plane_of(me), planes), slots)],
            send_sem=last_sem.at[0],
            recv_sem=last_sem.at[4 + lax.rem(plane_of(me), planes) // slots],
            device_id=at(source),
            device_id_type=MESH,
        )

    def last_own():
        return pltpu.make_async_copy(
            current, new_out.at[:, pl.ds(lax.rem(plane_of(me), planes), slots)], last_sem.at[0]
        )

    def point_back(target, sem):
        return pltpu.make_async_remote_copy(
            src_ref=current.at[:, 0, pl.ds(0, 8)],
            dst_ref=special_out,
            send_sem=last_sem.at[sem],
            recv_sem=last_sem.at[3],
            device_id=at(target),
            device_id_type=MESH,
        )

    @pl.when(source == me)
    def _():
        last_own().start()

    @pl.when(source != me)
    def _():
        last_sent().start()

    @pl.when(me == home)
    def _():
        point_back(0, 1).start()
        point_back(high_owner, 2).start()

    @pl.when(jnp.logical_and(me != 0, me != high_owner))
    def _():
        special_out[...] = jnp.zeros_like(special_out)

    @pl.when(jnp.logical_and(me * planes >= half // 2, me * planes < points - half // 2))
    def _():
        new_out[...] = jnp.zeros_like(new_out)

    def density(y, found):
        total = sum(f[:, :points] * f[:, :points] + f[:, points:] * f[:, points:] for f in found)
        part[y] = total * (2.0 / (bands * peers))

    space(density)

    def swap(i):
        return pltpu.make_async_remote_copy(
            src_ref=part,
            dst_ref=part_got.at[i - 1],
            send_sem=dens_sem.at[0, i - 1],
            recv_sem=dens_sem.at[1, i - 1],
            device_id={"band": lax.rem(band + i, peers), "grid": me},
            device_id_type=MESH,
        )

    for i in range(1, peers):
        swap(i).start()
    for i in range(1, peers):
        swap(i).wait()
    total = part[...] + core[...]
    for i in range(1, peers):
        total = total + part_got[i - 1]
    density_out[...] = total

    @pl.when(source == me)
    def _():
        last_own().wait()

    @pl.when(source != me)
    def _():
        last_sent().wait_send()

    @pl.when(me == home)
    def _():
        point_back(0, 1).wait_send()
        point_back(high_owner, 2).wait_send()

    @pl.when(jnp.logical_or(me == 0, me == high_owner))
    def _():
        point_back(home, 1).wait_recv()

    @pl.loop(0, n)
    def _(origin):
        @pl.when(jnp.logical_and(plane_of(origin) // planes == me, origin != me))
        def _():
            last_arrival(origin).wait_recv()


def update_bands(coefficients, potential, core, rotations):
    n, peers = lax.axis_size("grid"), lax.axis_size("band")
    bands, _, planes, points, _ = coefficients.shape
    iters = rotations.shape[0]
    half, quarter = points // 2, points // 4
    slots = half // n
    me = lax.axis_index("grid")

    def keep(value, axis):
        low = lax.slice_in_dim(value, 0, quarter, axis=axis)
        high = lax.slice_in_dim(value, points - quarter, points, axis=axis)
        return jnp.concatenate([low, high], axis)

    kept = keep(keep(coefficients, 3), 4)
    packed = jnp.concatenate([kept[:, 0], kept[:, 1]], -1)
    along_x = jnp.where(me == quarter // planes, coefficients[:, :, quarter % planes, 0, 0], 0.0)
    along_z = jnp.where(me == 0, coefficients[:, :, 0, 0, quarter], 0.0)
    along_y = jnp.where(me == 0, coefficients[:, :, 0, quarter, 0], 0.0)
    row = jnp.stack([jnp.zeros_like(along_x), along_x, along_z, along_y], -1)
    row = jnp.pad(row, ((0, 0), (0, 0), (0, half - 4))).reshape(bands, 1, points)
    lane = lax.iota(jnp.int32, points)
    zero_lane = (lane % half == 0).astype(F32)
    special = jnp.concatenate(
        [jnp.pad(row, ((0, 0), (0, 7), (0, 0))), jnp.broadcast_to(zero_lane, (bands, 8, points))], 1
    )

    def frequency(slot):
        return jnp.where(slot < quarter, slot, slot - half)

    gx = frequency(me * slots + lax.iota(jnp.int32, slots))[:, None, None]
    gy = frequency(lax.iota(jnp.int32, half))[None, :, None]
    gz = frequency(lane % half)[None, None, :]
    squared = gx * gx + gy * gy + gz * gz
    spot = (gx == -quarter) & (gy == 0) & (lane % half < 4)[None, None, :]
    squared = jnp.where(spot, quarter * quarter, squared)
    mask = (16 * squared <= points * points).astype(F32)
    kinetic = kinetic_scale * squared.astype(F32) / (points * points)

    rows = bands * half
    vmem = pl.BlockSpec(memory_space=pltpu.VMEM)
    smem = pl.BlockSpec(memory_space=pltpu.SMEM)
    stages = 2 * iters + 1
    chunk = (bands, slots, planes, points)
    gram_rows = -(-3 * bands * bands // 8) * 8
    dma = pltpu.SemaphoreType.DMA
    tables = band_tables(n, bands, points)
    y_phase = lax.dynamic_slice_in_dim(jnp.asarray(tables[-1]), me * planes, planes, 1)
    new, back, density = pl.pallas_call(
        functools.partial(band_kernel, n, peers, bands, points, iters),
        out_shape=(
            jax.ShapeDtypeStruct((bands, planes, half, points), F32),
            jax.ShapeDtypeStruct((bands, 8, points), F32),
            jax.ShapeDtypeStruct((planes, points, points), F32),
        ),
        in_specs=[vmem] * 6 + [smem] + [vmem] * (len(tables) + 1),
        out_specs=(vmem, vmem, vmem),
        scratch_shapes=[
            pltpu.VMEM((bands, slots, half, points), F32),
            pltpu.VMEM((bands, slots, half, points), F32),
            pltpu.VMEM((stages, n) + chunk, F32),
            pltpu.VMEM((stages, n) + chunk, F32),
            pltpu.VMEM((iters, gram_rows, points), F32),
            pltpu.VMEM((iters, n, gram_rows, points), F32),
            pltpu.VMEM(((rows + 8) * planes, points), F32),
            pltpu.VMEM(((rows + 8) * planes, points), F32),
            pltpu.VMEM((n,) + chunk, F32),
            pltpu.VMEM((2, bands, 16, points), F32),
            pltpu.VMEM((planes, points, points), F32),
            pltpu.VMEM((max(peers - 1, 1), planes, points, points), F32),
            dma((stages, n)),
            dma((stages, n)),
            dma((iters, n)),
            dma((iters, n)),
            dma((5 + planes // slots,)),
            dma((4 + planes // slots,)),
            dma((2, max(peers - 1, 1))),
        ],
        compiler_params=pltpu.CompilerParams(
            collective_id=0, has_side_effects=True, vmem_limit_bytes=60 * 2**20
        ),
    )(packed, special, mask, kinetic, potential, core, rotations, *tables, y_phase)

    parts = jnp.stack([new[..., :half], new[..., half:]], 1)

    def widen(value, axis):
        low = lax.slice_in_dim(value, 0, quarter, axis=axis)
        high = lax.slice_in_dim(value, quarter, half, axis=axis)
        shape = list(value.shape)
        shape[axis] = points - half
        return jnp.concatenate([low, jnp.zeros(shape, F32), high], axis)

    gx_own = me * planes + lax.iota(jnp.int32, planes)
    live = (gx_own != points - quarter)[:, None, None] | (
        (lax.iota(jnp.int32, half) == 0)[None, :, None] & (lax.iota(jnp.int32, half) == 0)[None, None, :]
    )
    kept_plane = ((gx_own < quarter) | (gx_own >= points - quarter))[:, None, None]
    wide = widen(widen(jnp.where(live & kept_plane, parts, 0.0), 3), 4)
    found = back[:, 0].reshape(bands, 2, half)
    i_x = lax.broadcasted_iota(jnp.int32, (1, 1, planes, points, points), 2) + me * planes
    i_y = lax.broadcasted_iota(jnp.int32, (1, 1, planes, points, points), 3)
    i_z = lax.broadcasted_iota(jnp.int32, (1, 1, planes, points, points), 4)

    def spread(k):
        return found[:, :, k][:, :, None, None, None]

    wide = jnp.where((i_x == quarter) & (i_y == 0) & (i_z == 0), spread(1), wide)
    wide = jnp.where((i_x == 0) & (i_y == 0) & (i_z == quarter), spread(2), wide)
    wide = jnp.where((i_x == 0) & (i_y == quarter) & (i_z == 0), spread(3), wide)
    return wide, density


def frequencies(points, offset, length):
    places = offset + lax.iota(jnp.int32, length)
    return jnp.where(2 * places < points, places, places - points)


def reciprocal_tables(points, offset, length):
    along_x = frequencies(points, offset, length)
    along = frequencies(points, 0, points)
    squared = (
        along_x[:, None, None] * along_x[:, None, None]
        + along[None, :, None] * along[None, :, None]
        + along[None, None, :] * along[None, None, :]
    )
    return jnp.where(
        squared > 0, coulomb_scale * (points * points) / jnp.maximum(squared, 1).astype(F32), 0.0
    )


def full_dot(a, b):
    return jnp.dot(a, b, preferred_element_type=F32, precision=lax.Precision.HIGHEST)


def field_kernel(
    n, points, hidden,
    density, cube, external, coulomb, basis, slope, slope_t, mlp_in, mlp_out, out,
    sent, got, back_h, back_y, got_h, got_y, send_sem, recv_sem,
):
    me = lax.axis_index("grid")
    band = lax.axis_index("band")
    planes = points // n
    block = planes * planes

    barrier = pltpu.get_barrier_semaphore()

    @pl.loop(1, n)
    def _(i):
        pl.semaphore_signal(
            barrier, inc=1, device_id={"band": band, "grid": lax.rem(me + i, n)}, device_id_type=MESH
        )

    def exchange(pairs):
        def copy(k, target, origin):
            source, place = pairs[k][1:]
            return pltpu.make_async_remote_copy(
                src_ref=source.at[target],
                dst_ref=place.at[pl.ds(origin * block, block)],
                send_sem=send_sem.at[pairs[k][0], target],
                recv_sem=recv_sem.at[pairs[k][0], origin],
                device_id={"band": band, "grid": target},
                device_id_type=MESH,
            )

        @pl.loop(1, n)
        def _(i):
            for k in range(len(pairs)):
                copy(k, lax.rem(me + i, n), me).start()

        for stage, source, place in pairs:
            own = pltpu.make_async_copy(
                source.at[me], place.at[pl.ds(me * block, block)], recv_sem.at[stage, me]
            )
            own.start()
            own.wait()

        @pl.loop(1, n)
        def _(i):
            origin = lax.rem(me + n - i, n)
            for k in range(len(pairs)):
                copy(k, lax.rem(me + i, n), me).wait_send()
                copy(k, origin, origin).wait_recv()

    for y in range(planes):
        level = full_dot(full_dot(basis[...], density[y] - 2.275), basis[...])
        out[pl.ds(y, points, stride=planes), :] = level
    sent[...] = out[...].reshape(n, block, points)
    pl.semaphore_wait(barrier, n - 1)
    exchange([(0, sent, got)])
    arrived = got[...].reshape(n, planes, planes, points)
    for x in range(planes):
        column = arrived[:, x].reshape(points, points)
        weighted = coulomb[x] * full_dot(basis[...], column)
        back_h[:, x * planes : (x + 1) * planes] = full_dot(basis[...], weighted).reshape(n, planes, points)
        back_y[:, x * planes : (x + 1) * planes] = full_dot(slope[...], column).reshape(n, planes, points)
    exchange([(1, back_h, got_h), (2, back_y, got_y)])

    for y in range(planes):
        hartree = full_dot(full_dot(basis[...], got_h[pl.ds(y, points, stride=planes), :]), basis[...])
        change_y = full_dot(full_dot(basis[...], got_y[pl.ds(y, points, stride=planes), :]), basis[...])
        change_y = change_y * (1.0 / (points * points))
        varying = density[y] - 2.275
        change_x = full_dot(slope[...], varying)
        change_z = full_dot(varying, slope_t[...])
        gradient = jnp.sqrt(change_x * change_x + change_y * change_y + change_z * change_z)
        root = cube[y]
        reduced = gradient / (reduced_scale * density[y] * root)
        bounded = reduced / (1.0 + reduced)

        def unit(k, total):
            return total + mlp_out[k] * jnp.tanh(mlp_in[0, k] * root + mlp_in[1, k] * bounded + mlp_in[2, k])

        enhance = lax.fori_loop(0, hidden, unit, jnp.ones_like(root))
        out[y * points : (y + 1) * points, :] = (
            external[y] + hartree - exchange_scale * root * enhance
        )


def body(coefficients, potential, external, core_density, rotations, mlp_in, mlp_out):
    points = potential.shape[1]
    planes = coefficients.shape[2]
    n = lax.axis_size("grid")
    offset = lax.axis_index("grid") * planes
    coulomb = reciprocal_tables(points, offset, planes) * (1.0 / points**3)
    current, density = update_bands(coefficients, potential, core_density, rotations)

    cell = np.arange(points)
    angle = 2.0 * np.pi * ((cell[:, None] * cell[None, :]) % points) / points
    freq = np.where(2 * cell < points, cell, cell - points)
    slope = gradient_scale * np.where(2 * freq == -points, 0, freq) / points
    back = (np.exp(1j * angle) * slope[None, :] * 1j) @ np.exp(-1j * angle) / points
    slope_table = np.ascontiguousarray(back.real).astype(np.float32)
    basis = (np.cos(angle) + np.sin(angle)).astype(np.float32)
    vmem = pl.BlockSpec(memory_space=pltpu.VMEM)
    smem = pl.BlockSpec(memory_space=pltpu.SMEM)
    block = planes * planes
    new_potential = pl.pallas_call(
        functools.partial(field_kernel, n, points, mlp_out.shape[0]),
        out_shape=jax.ShapeDtypeStruct((planes * points, points), F32),
        in_specs=[vmem] * 7 + [smem, smem],
        out_specs=vmem,
        scratch_shapes=[
            pltpu.VMEM((n, block, points), F32),
            pltpu.VMEM((n * block, points), F32),
            pltpu.VMEM((n, block, points), F32),
            pltpu.VMEM((n, block, points), F32),
            pltpu.VMEM((n * block, points), F32),
            pltpu.VMEM((n * block, points), F32),
            pltpu.SemaphoreType.DMA((3, n)),
            pltpu.SemaphoreType.DMA((3, n)),
        ],
        compiler_params=pltpu.CompilerParams(
            collective_id=1, has_side_effects=True, vmem_limit_bytes=40 * 2**20
        ),
    )(density, jnp.cbrt(density), external, coulomb, basis, slope_table, slope_table.T.copy(), mlp_in, mlp_out)
    return (current, new_potential.reshape(planes, points, points))


def solution(mesh):
    in_specs = (
        P("band", None, "grid", None, None),
        P("grid", None, None),
        P("grid", None, None),
        P("grid", None, None),
        P(None, "band", None),
        P(),
        P(),
    )
    out_specs = (P("band", None, "grid", None, None), P("grid", None, None))
    return jax.shard_map(body, mesh=mesh, in_specs=in_specs, out_specs=out_specs, check_vma=False)
```

profile of v0, /device:TPU:12, one launch (start us, length us, event | category | flops | bytes accessed | tf_op | source)
XLA Modules:
  0.0 185.6 jit_solution(13664922661128852396)
XLA Ops:
  0.8 0.1 broadcast_and_fusion.1
  1.0 1.0 fusion.10
  2.1 0.1 copy.43
  2.2 0.1 reshape.284
  2.3 0.6 select_maximum_fusion.special
  3.0 1.3 constant_dynamic-slice_fusion.y_phase
  4.3 0.1 or_and_fusion
  4.4 0.8 convert_multiply_fusion.kinetic
  5.2 0.8 fusion.9.mask
  6.0 0.3 and_and_fusion.2
  6.3 0.2 fusion.5.coulomb
  6.6 1.3 fusion.22
  7.9 0.4 slice_maximum_fusion
  8.2 0.3 fusion.7
  8.6 1.0 pad_maximum_fusion.3.packed
  9.6 105.1 %shard_map.203 = (f32[2,8,64,128]{3,2,1,0:T(8,128)}, f32[2,8,128]{2,1,0:T(8,128)}, f32[8,128,128]{2,1,0:T(8,128)}) custom-call(f32[2,8,64,128]{3,2,1,0:T(8,128)} %pad_maximum_fusion.3.packed, f32[2,16,128]{2,1,0:T(8,128)} %select_maximum_fusion.special, f32[4,64,128]{2,1,0:T(8,128)} %fusion.9.mask, f32[4,64,128]{2,1,0:T(8,128)} %convert_multiply_fusion.kinetic, ...), custom_call_target="tpu_custom_call" | custom-call | tf_op jit(solution)/shard_map/pallas_call | solution.py:549
  114.7 0.8 slice_reduce_fusion
  115.5 0.1 reshape_squeeze.3
  115.6 0.1 fusion.24
  115.7 0.1 copy.40
  115.8 0.1 copy.41
  115.9 0.1 copy.42
  116.0 1.4 cbrt.3.cube
  117.5 1.0 copy-done
  118.5 62.7 %shard_map.204 = f32[1024,128]{1,0:T(8,128)S(1)} custom-call(f32[8,128,128]{2,1,0:T(8,128)S(1)} %copy-done, f32[8,128,128]{2,1,0:T(8,128)S(1)} %cbrt.3.cube, f32[8,128,128]{2,1,0:T(8,128)S(1)} %copy-done.1, f32[8,128,128]{2,1,0:T(8,128)S(1)} %fusion.5.coulomb, f32[128,128]{1,0:T(8,128)S(1)} %copy-done.4, f32[128,128]{1,0:T(8,128)S(1)} %copy-done.3, ...), custom_call_target="tpu_custom_call" | custom-call | tf_op jit(solution)/shard_map/pallas_call | solution.py:737
  181.2 0.2 slice_bitcast_fusion.1
  181.4 0.2 maximum_select_fusion.1
  181.7 0.1 broadcast_in_dim.95
  181.8 0.2 pad_maximum_fusion
  182.0 0.7 fusion.21
  182.7 2.1 %fusion.1 = f32[2,2,8,128,128]{4,3,2,1,0:T(8,128)} fusion(f32[128]{0:T(128)S(1)} %pad.11.clone, f32[2,2]{1,0:T(2,128)S(1)} %bitcast.22, f32[2,2]{1,0:T(2,128)S(1)} %bitcast.21, f32[2,2]{1,0:T(2,128)S(1)} %bitcast.20, pred[8,128,128]{2,1,0:T(8,128)(4,1)S(1)} %get-tuple-element.28, pred[8,128,128]{2,1,0:T(8,128)(4,1)S(1)} %get-tuple-element.27, ...), kind=kLoop, calls=%fused_computation.3 | loop fusion | flops 2621440 | bytes 3539504 | tf_op jit(solution)/shard_map/jit(_where)/select_n | solution.py:609
  184.8 0.8 copy.56
  (38 shorter events, 0.6 us)
Async XLA Ops:
  9.6 107.8 %copy-start.1 = (f32[8,128,128]{2,1,0:T(8,128)S(1)}, f32[8,128,128]{2,1,0:T(8,128)}, u32[]{:S(2)}) copy-start(f32[8,128,128]{2,1,0:T(8,128)} %external.1) | copy-start | bytes 1572868
  9.6 107.8 %copy-start.2 = (f32[128,128]{1,0:T(8,128)S(1)}, f32[128,128]{1,0:T(8,128)}, u32[]{:S(2)}) copy-start(f32[128,128]{1,0:T(8,128)} %constant.128.clone.slope_t) | copy-start | bytes 196612
  9.6 107.9 %copy-start.3 = (f32[128,128]{1,0:T(8,128)S(1)}, f32[128,128]{1,0:T(8,128)}, u32[]{:S(2)}) copy-start(f32[128,128]{1,0:T(8,128)} %constant.127.clone.slope) | copy-start | bytes 196612
  9.6 107.9 %copy-start.4 = (f32[128,128]{1,0:T(8,128)S(1)}, f32[128,128]{1,0:T(8,128)}, u32[]{:S(2)}) copy-start(f32[128,128]{1,0:T(8,128)} %constant.126.clone.basis) | copy-start | bytes 196612
  9.6 107.9 %copy-start.5 = (f32[3,32]{1,0:T(4,128)S(1)}, f32[3,32]{1,0:T(4,128)}, u32[]{:S(2)}) copy-start(f32[3,32]{1,0:T(4,128)} %mlp_in.1) | copy-start | bytes 1156
  9.6 107.9 %copy-start.6 = (f32[32]{0:T(128)S(1)}, f32[32]{0:T(128)}, u32[]{:S(2)}) copy-start(f32[32]{0:T(128)} %mlp_out.1) | copy-start | bytes 388
  114.7 66.5 %copy-start.7 = (f32[2,8,64,128]{3,2,1,0:T(8,128)S(1)}, f32[2,8,64,128]{3,2,1,0:T(8,128)}, u32[]{:S(2)}) copy-start(f32[2,8,64,128]{3,2,1,0:T(8,128)} %get-tuple-element.6) | copy-start | bytes 1572868
  117.5 1.0 copy-start
where the time goes:
time: 187 us; the launch traced here: 186 us
  Pallas kernels  168 us (90%)
  local copies, waits for them, and re-layouts  8.52 us (5%)
  other arithmetic  8.4 us (4%)
    pallas_call x1, Pallas kernels, update_bands(): pl.pallas_call(functools.partial(band_kernel, n, peers, bands, points, it...  105 us
    pallas_call x1, Pallas kernels, body(): pl.pallas_call(functools.partial(field_kernel, n, points, mlp_out.shape[0...  62.7 us

commit v1 on v0

--- a/solution.py
+++ b/solution.py
@@ -633,9 +633,9 @@
 
 
 def field_kernel(
-    n, points, hidden,
-    density, cube, external, coulomb, basis, slope, slope_t, mlp_in, mlp_out, out,
-    sent, got, back_h, back_y, got_h, got_y, send_sem, recv_sem,
+    n, peers, points, hidden,
+    density, cube, external, coulomb, basis, basis_2, slope_2, slope_t2, mlp_in, mlp_out, out,
+    staged, sent, got, back_h, back_y, got_h, got_y, send_sem, recv_sem, share_sem,
 ):
     me = lax.axis_index("grid")
     band = lax.axis_index("band")
@@ -648,6 +648,13 @@
     def _(i):
         pl.semaphore_signal(
             barrier, inc=1, device_id={"band": band, "grid": lax.rem(me + i, n)}, device_id_type=MESH
+        )
+
+    share = planes // peers if planes % peers == 0 else planes
+    others = range(1, peers) if share < planes else range(0)
+    for i in others:
+        pl.semaphore_signal(
+            barrier, inc=1, device_id={"band": lax.rem(band + i, peers), "grid": me}, device_id_type=MESH
         )
 
     def exchange(pairs):
@@ -683,25 +690,31 @@
 
     for y in range(planes):
         level = full_dot(full_dot(basis[...], density[y] - 2.275), basis[...])
-        out[pl.ds(y, points, stride=planes), :] = level
-    sent[...] = out[...].reshape(n, block, points)
-    pl.semaphore_wait(barrier, n - 1)
+        staged[pl.ds(y, points, stride=planes), :] = level
+    sent[...] = staged[...].reshape(n, block, points)
+    pl.semaphore_wait(barrier, n - 1 + len(others))
     exchange([(0, sent, got)])
     arrived = got[...].reshape(n, planes, planes, points)
     for x in range(planes):
         column = arrived[:, x].reshape(points, points)
         weighted = coulomb[x] * full_dot(basis[...], column)
-        back_h[:, x * planes : (x + 1) * planes] = full_dot(basis[...], weighted).reshape(n, planes, points)
-        back_y[:, x * planes : (x + 1) * planes] = full_dot(slope[...], column).reshape(n, planes, points)
+        back_h[:, x * planes : (x + 1) * planes] = table_left(basis_2, weighted).reshape(n, planes, points)
+        back_y[:, x * planes : (x + 1) * planes] = table_left(slope_2, column).reshape(n, planes, points)
     exchange([(1, back_h, got_h), (2, back_y, got_y)])
 
-    for y in range(planes):
-        hartree = full_dot(full_dot(basis[...], got_h[pl.ds(y, points, stride=planes), :]), basis[...])
-        change_y = full_dot(full_dot(basis[...], got_y[pl.ds(y, points, stride=planes), :]), basis[...])
-        change_y = change_y * (1.0 / (points * points))
+    first = band * share if share < planes else 0
+    for i in range(share):
+        y = first + i
+        both = jnp.concatenate(
+            [got_h[pl.ds(y, points, stride=planes), :], got_y[pl.ds(y, points, stride=planes), :]], 1
+        )
+        both = table_left(basis_2, both)
+        both = table_right(jnp.concatenate([both[:, :points], both[:, points:]], 0), basis_2)
+        hartree = both[:points]
+        change_y = both[points:] * (1.0 / (points * points))
         varying = density[y] - 2.275
-        change_x = full_dot(slope[...], varying)
-        change_z = full_dot(varying, slope_t[...])
+        change_x = table_left(slope_2, varying)
+        change_z = table_right(varying, slope_t2)
         gradient = jnp.sqrt(change_x * change_x + change_y * change_y + change_z * change_z)
         root = cube[y]
         reduced = gradient / (reduced_scale * density[y] * root)
@@ -710,16 +723,31 @@
         def unit(k, total):
             return total + mlp_out[k] * jnp.tanh(mlp_in[0, k] * root + mlp_in[1, k] * bounded + mlp_in[2, k])
 
-        enhance = lax.fori_loop(0, hidden, unit, jnp.ones_like(root))
-        out[y * points : (y + 1) * points, :] = (
-            external[y] + hartree - exchange_scale * root * enhance
-        )
+        enhance = lax.fori_loop(0, hidden, unit, jnp.ones_like(root), unroll=4)
+        out[y] = external[y] + hartree - exchange_scale * root * enhance
+
+    def shared(i, whose):
+        part = out.at[pl.ds(whose * share, share)]
+        return pltpu.make_async_remote_copy(
+            src_ref=part,
+            dst_ref=part,
+            send_sem=share_sem.at[0, i - 1],
+            recv_sem=share_sem.at[1, i - 1],
+            device_id={"band": lax.rem(band + i, peers), "grid": me},
+            device_id_type=MESH,
+        )
+
+    for i in others:
+        shared(i, band).start()
+    for i in others:
+        shared(i, band).wait_send()
+        shared(i, lax.rem(band + peers - i, peers)).wait_recv()
 
 
 def body(coefficients, potential, external, core_density, rotations, mlp_in, mlp_out):
     points = potential.shape[1]
     planes = coefficients.shape[2]
-    n = lax.axis_size("grid")
+    n, peers = lax.axis_size("grid"), lax.axis_size("band")
     offset = lax.axis_index("grid") * planes
     coulomb = reciprocal_tables(points, offset, planes) * (1.0 / points**3)
     current, density = update_bands(coefficients, potential, core_density, rotations)
@@ -735,11 +763,12 @@
     smem = pl.BlockSpec(memory_space=pltpu.SMEM)
     block = planes * planes
     new_potential = pl.pallas_call(
-        functools.partial(field_kernel, n, points, mlp_out.shape[0]),
-        out_shape=jax.ShapeDtypeStruct((planes * points, points), F32),
-        in_specs=[vmem] * 7 + [smem, smem],
+        functools.partial(field_kernel, n, peers, points, mlp_out.shape[0]),
+        out_shape=jax.ShapeDtypeStruct((planes, points, points), F32),
+        in_specs=[vmem] * 8 + [smem, smem],
         out_specs=vmem,
         scratch_shapes=[
+            pltpu.VMEM((n * block, points), F32),
             pltpu.VMEM((n, block, points), F32),
             pltpu.VMEM((n * block, points), F32),
             pltpu.VMEM((n, block, points), F32),
@@ -748,12 +777,16 @@
             pltpu.VMEM((n * block, points), F32),
             pltpu.SemaphoreType.DMA((3, n)),
             pltpu.SemaphoreType.DMA((3, n)),
+            pltpu.SemaphoreType.DMA((2, max(peers - 1, 1))),
         ],
         compiler_params=pltpu.CompilerParams(
             collective_id=1, has_side_effects=True, vmem_limit_bytes=40 * 2**20
         ),
-    )(density, jnp.cbrt(density), external, coulomb, basis, slope_table, slope_table.T.copy(), mlp_in, mlp_out)
-    return (current, new_potential.reshape(planes, points, points))
+    )(
+        density, jnp.cbrt(density), external, coulomb, basis,
+        halves(basis), halves(slope_table), halves(slope_table.T), mlp_in, mlp_out,
+    )
+    return (current, new_potential)
 
 
 def solution(mesh):

time: 187 us -> 179 us (0.957)
  Pallas kernels: 168 us -> 160 us
    pallas_call x1, Pallas kernels: 62.7 us -> 54.2 us  [body(): pl.pallas_call(functools.partial(field_kernel, n, peers, points, mlp_out....]
where the time goes in v1:
time: 179 us; the launch traced here: 177 us
  Pallas kernels  160 us (89%)
  local copies, waits for them, and re-layouts  8.52 us (5%)
  other arithmetic  8.39 us (5%)
    pallas_call x1, Pallas kernels, update_bands(): pl.pallas_call(functools.partial(band_kernel, n, peers, bands, points, it...  105 us
    pallas_call x1, Pallas kernels, body(): pl.pallas_call(functools.partial(field_kernel, n, peers, points, mlp_out....  54.2 us

profile of v1, /device:TPU:12, one launch (start us, length us, event | category | flops | bytes accessed | tf_op | source)
XLA Modules:
  0.0 177.4 jit_solution(3674439668054558350)
XLA Ops:
  0.8 0.1 broadcast_and_fusion.1
  1.0 1.0 fusion.10
  2.1 0.1 copy.44
  2.2 0.1 reshape.281
  2.3 0.6 select_maximum_fusion.special
  3.0 1.3 constant_dynamic-slice_fusion.y_phase
  4.3 0.1 or_and_fusion
  4.4 0.8 convert_multiply_fusion.kinetic
  5.2 0.8 fusion.9.mask
  6.0 0.3 and_and_fusion.2
  6.3 0.2 fusion.5.coulomb
  6.6 1.3 fusion.22
  7.8 0.4 slice_maximum_fusion
  8.2 0.3 fusion.7
  8.6 1.0 pad_maximum_fusion.3.packed
  9.6 105.4 %shard_map.212 = (f32[2,8,64,128]{3,2,1,0:T(8,128)}, f32[2,8,128]{2,1,0:T(8,128)}, f32[8,128,128]{2,1,0:T(8,128)}) custom-call(f32[2,8,64,128]{3,2,1,0:T(8,128)} %pad_maximum_fusion.3.packed, f32[2,16,128]{2,1,0:T(8,128)} %select_maximum_fusion.special, f32[4,64,128]{2,1,0:T(8,128)} %fusion.9.mask, f32[4,64,128]{2,1,0:T(8,128)} %convert_multiply_fusion.kinetic, ...), custom_call_target="tpu_custom_call" | custom-call | tf_op jit(solution)/shard_map/pallas_call | solution.py:549
  115.1 0.8 slice_reduce_fusion
  115.8 0.1 reshape_squeeze.3
  115.9 0.1 fusion.24
  116.0 0.1 copy.41
  116.1 0.1 copy.42
  116.2 0.1 copy.43
  116.3 1.4 cbrt.3.cube
  117.8 1.0 copy-done
  118.9 54.2 %shard_map.213 = f32[8,128,128]{2,1,0:T(8,128)S(1)} custom-call(f32[8,128,128]{2,1,0:T(8,128)S(1)} %copy-done, f32[8,128,128]{2,1,0:T(8,128)S(1)} %cbrt.3.cube, f32[8,128,128]{2,1,0:T(8,128)S(1)} %copy-done.1, f32[8,128,128]{2,1,0:T(8,128)S(1)} %fusion.5.coulomb, f32[128,128]{1,0:T(8,128)S(1)} %copy-done.5, bf16[2,128,128]{2,1,0:T(8,128)(2,1)S(1)} %copy-done.4, ...), custom_call_target="tpu_custom_call" | custom-call | tf_op jit(solution)/shard_map/pallas_call | solution.py:765
  173.1 0.2 slice_bitcast_fusion.1
  173.3 0.2 maximum_select_fusion.1
  173.5 0.1 broadcast_in_dim.95
  173.6 0.2 pad_maximum_fusion
  173.8 0.7 fusion.21
  174.6 2.1 %fusion.1 = f32[2,2,8,128,128]{4,3,2,1,0:T(8,128)} fusion(f32[128]{0:T(128)S(1)} %pad.11.clone, f32[2,2]{1,0:T(2,128)S(1)} %bitcast.20, f32[2,2]{1,0:T(2,128)S(1)} %bitcast.19, f32[2,2]{1,0:T(2,128)S(1)} %bitcast.18, pred[8,128,128]{2,1,0:T(8,128)(4,1)S(1)} %get-tuple-element.28, pred[8,128,128]{2,1,0:T(8,128)(4,1)S(1)} %get-tuple-element.27, ...), kind=kLoop, calls=%fused_computation.3 | loop fusion | flops 2621440 | bytes 3539504 | tf_op jit(solution)/shard_map/jit(_where)/select_n | solution.py:609
  176.7 0.8 copy.57
  (40 shorter events, 0.6 us)
Async XLA Ops:
  9.6 108.2 %copy-start.1 = (f32[8,128,128]{2,1,0:T(8,128)S(1)}, f32[8,128,128]{2,1,0:T(8,128)}, u32[]{:S(2)}) copy-start(f32[8,128,128]{2,1,0:T(8,128)} %external.1) | copy-start | bytes 1572868
  9.6 108.2 %copy-start.2 = (bf16[2,128,128]{2,1,0:T(8,128)(2,1)S(1)}, bf16[2,128,128]{2,1,0:T(8,128)(2,1)}, u32[]{:S(2)}) copy-start(bf16[2,128,128]{2,1,0:T(8,128)(2,1)} %constant.131.clone.slope_t2) | copy-start | bytes 196612
  9.6 108.2 %copy-start.3 = (bf16[2,128,128]{2,1,0:T(8,128)(2,1)S(1)}, bf16[2,128,128]{2,1,0:T(8,128)(2,1)}, u32[]{:S(2)}) copy-start(bf16[2,128,128]{2,1,0:T(8,128)(2,1)} %constant.130.clone.slope_2) | copy-start | bytes 196612
  9.6 108.2 %copy-start.4 = (bf16[2,128,128]{2,1,0:T(8,128)(2,1)S(1)}, bf16[2,128,128]{2,1,0:T(8,128)(2,1)}, u32[]{:S(2)}) copy-start(bf16[2,128,128]{2,1,0:T(8,128)(2,1)} %constant.129.clone.basis_2) | copy-start | bytes 196612
  9.6 108.2 %copy-start.5 = (f32[128,128]{1,0:T(8,128)S(1)}, f32[128,128]{1,0:T(8,128)}, u32[]{:S(2)}) copy-start(f32[128,128]{1,0:T(8,128)} %constant.128.clone.basis) | copy-start | bytes 196612
  9.6 108.2 %copy-start.6 = (f32[3,32]{1,0:T(4,128)S(1)}, f32[3,32]{1,0:T(4,128)}, u32[]{:S(2)}) copy-start(f32[3,32]{1,0:T(4,128)} %mlp_in.1) | copy-start | bytes 1156
  9.6 108.2 %copy-start.7 = (f32[32]{0:T(128)S(1)}, f32[32]{0:T(128)}, u32[]{:S(2)}) copy-start(f32[32]{0:T(128)} %mlp_out.1) | copy-start | bytes 388
  115.1 58.0 %copy-start.8 = (f32[2,8,64,128]{3,2,1,0:T(8,128)S(1)}, f32[2,8,64,128]{3,2,1,0:T(8,128)}, u32[]{:S(2)}) copy-start(f32[2,8,64,128]{3,2,1,0:T(8,128)} %get-tuple-element.6) | copy-start | bytes 1572868
  117.8 1.0 copy-start
